TPU v7x, 256 devices: a whole 4x4x8 slice. The times are simulated.
256 devices in a mesh: tm: 16 (over x, y), space: 16 (over z, core).
Axes of the slice: x: 4, y: 4, z: 8, core: 2. Of those that a mesh axis runs over, the one named last changes fastest.
Arguments:
- clip: bfloat16 [256, 512, 768], P('tm', 'space'), may hold values from -160 to 160
- w_spatial: bfloat16 [4, 768, 768], replicated, may hold values from -4 to 4
- w_temporal: bfloat16 [4, 768, 768], replicated, may hold values from -4 to 4
Outputs:
- result: bfloat16 [256, 512, 768], P('tm', 'space')
All inputs are finite; a program needn't handle non-finite values.
Results may differ from a plain program's by a relative error of at most 0.011.
Values may be sent and summed in bfloat16 or wider, within the bound.
A program may use at most 128 MiB of HBM per device.

v0:
```python
import math
import jax
import jax.numpy as jnp
from jax import lax
from jax.sharding import PartitionSpec as P

HEAD = 64


def rms_norm(values):
    wide = values.astype(jnp.float32)
    return (wide * lax.rsqrt(jnp.mean(wide * wide, axis=-1, keepdims=True) + 1e-06)).astype(
        jnp.bfloat16
    )


def project_three(normed, weights):
    width = normed.shape[-1]
    flat = normed.reshape(-1, width)
    stacked = jnp.einsum(
        "rd,jde->jre", flat, weights[:3], preferred_element_type=jnp.float32
    ).astype(jnp.bfloat16)
    return (
        stacked[0].reshape(normed.shape),
        stacked[1].reshape(normed.shape),
        stacked[2].reshape(normed.shape),
    )


def out_project(mixed, weight):
    width = mixed.shape[-1]
    return jnp.dot(mixed.reshape(-1, width), weight, preferred_element_type=jnp.float32).reshape(
        mixed.shape
    )


def attend_frame(parts):
    query, key, value = parts
    count, width = query.shape
    heads = width // HEAD
    qh = query.reshape(count, heads, HEAD)
    kh = key.reshape(count, heads, HEAD)
    vh = value.reshape(count, heads, HEAD)
    scores = jnp.einsum("qhd,khd->hqk", qh, kh, preferred_element_type=jnp.float32) * (
        1.0 / math.sqrt(HEAD)
    )
    largest = jnp.max(scores, axis=-1, keepdims=True)
    expo = jnp.exp(scores - largest)
    weights = (expo / jnp.sum(expo, axis=-1, keepdims=True)).astype(jnp.bfloat16)
    mixed = jnp.einsum("hqk,khd->qhd", weights, vh, preferred_element_type=jnp.float32)
    return mixed.astype(jnp.bfloat16).reshape(count, width)


def frame_block(parts):
    inner = (parts[0][0], parts[1][0], parts[2][0])
    return lax.map(attend_frame, inner)[None]


def on_device(clip, w_spatial, w_temporal):
    frames, toks, width = clip.shape
    heads = width // HEAD
    space_count = lax.axis_size("space")
    frame_shape = (space_count, frames // space_count, toks, width)
    normed = rms_norm(clip)
    sq, sk, sv = project_three(normed, w_spatial)
    smix = frame_block(
        (
            lax.all_to_all(
                sq.reshape(frame_shape), "space", split_axis=0, concat_axis=2, tiled=True
            ),
            lax.all_to_all(
                sk.reshape(frame_shape), "space", split_axis=0, concat_axis=2, tiled=True
            ),
            lax.all_to_all(
                sv.reshape(frame_shape), "space", split_axis=0, concat_axis=2, tiled=True
            ),
        )
    )
    smix = lax.all_to_all(smix, "space", split_axis=2, concat_axis=0, tiled=True).reshape(
        frames, toks, width
    )
    after_space = (clip.astype(jnp.float32) + out_project(smix, w_spatial[3])).astype(jnp.bfloat16)
    tnormed = rms_norm(after_space)
    tq, tk, tv = project_three(tnormed, w_temporal)
    first_frame = lax.axis_index("tm") * frames
    qh = tq.reshape(frames, toks, heads, HEAD)
    query_pos = first_frame + jnp.arange(frames, dtype=jnp.int32)
    running = jnp.full((frames, toks, heads), -1e30, jnp.float32)
    key_piece = lax.all_gather(tk, "tm", axis=0, tiled=True)
    value_piece = lax.all_gather(tv, "tm", axis=0, tiled=True)
    count = key_piece.shape[0]
    kh = key_piece.reshape(count, toks, heads, HEAD)
    vh = value_piece.reshape(count, toks, heads, HEAD)
    scores = jnp.einsum("fphd,gphd->fphg", qh, kh, preferred_element_type=jnp.float32) * (
        1.0 / math.sqrt(HEAD)
    )
    key_pos = jnp.arange(count, dtype=jnp.int32)
    allowed = (key_pos[None, :] <= query_pos[:, None])[:, None, None, :]
    scores = jnp.where(allowed, scores, -1e30)
    newmax = jnp.maximum(running, jnp.max(scores, axis=-1))
    expo = jnp.where(allowed, jnp.exp(scores - newmax[..., None]), 0.0)
    total = jnp.sum(expo, axis=-1)
    acc = jnp.einsum("fphg,gphd->fphd", expo, vh.astype(jnp.float32))
    running, total, acc = (newmax, total, acc)
    tmix = (acc / total[..., None]).reshape(frames, toks, width).astype(jnp.bfloat16)
    return (after_space.astype(jnp.float32) + out_project(tmix, w_temporal[3])).astype(jnp.bfloat16)


def solution(mesh):
    placed = (P("tm", "space", None), P(), P())
    return jax.shard_map(
        on_device, mesh=mesh, in_specs=placed, out_specs=P("tm", "space", None), check_vma=False
    )
```

profile of v0, /device:TPU:1, one launch (start us, length us, event | category | flops | bytes accessed | tf_op | source)
XLA Modules:
  0.0 389.2 jit_solution(14649983245477244457)
XLA Ops:
  6.5 1.4 fusion.23
  7.9 1.3 fusion.24
  9.2 4.0 %convert_bitcast_fusion.1 = bf16[3,512,768]{2,1,0:T(8,128)(2,1)S(1)} fusion(bf16[512,768,1]{1,0,2:T(8,128)(2,1)S(1)} %bitcast.74, bf16[4,768,768]{2,1,0:T(8,128)(2,1)} %param.4), kind=kOutput, calls=%fused_computation.30 | convolution fusion | flops 1813118976 | bytes 6684672 | tf_op jit(solution)/shard_map/rd,jde->jre/dot_general | solution.py:20
  13.3 1.0 fusion.54
  14.3 32.7 %all_to_all.16 = bf16[16,1,32,768]{3,2,1,0:T(8,128)(2,1)} all-to-all(bf16[16,1,32,768]{3,2,1,0:T(8,128)(2,1)S(1)} %bitcast.73), channel_id=1, replica_groups=mesh['tm'=16,'space'=16] {'space'}, dimensions={0} | all-to-all | bytes 1572864 | tf_op jit(solution)/shard_map/all_to_all | solution.py:68
  47.0 25.7 %all_to_all.17 = bf16[16,1,32,768]{3,2,1,0:T(8,128)(2,1)} all-to-all(bf16[16,1,32,768]{3,2,1,0:T(8,128)(2,1)S(1)} %bitcast.72), channel_id=1, replica_groups=mesh['tm'=16,'space'=16] {'space'}, dimensions={0} | all-to-all | bytes 1572864 | tf_op jit(solution)/shard_map/all_to_all | solution.py:71
  72.7 3.5 all-to-all-start
  76.2 0.2 all-gather.5.cloned.1.call-start
  76.4 2.7 reshape.105
  79.1 3.8 reshape.106
  82.9 8.0 %fusion.32 = f32[12,512,512]{1,2,0:T(8,128)} fusion(bf16[512,12,64]{2,1,0:T(8,128)(2,1)} %reshape.106, bf16[512,12,64]{2,1,0:T(8,128)(2,1)S(1)} %reshape.105), kind=kOutput, calls=%fused_computation.40 | convolution fusion | flops 402653184 | bytes 14155776 | tf_op jit(solution)/shard_map/while/body/eval_jaxpr/qhd,khd->hqk/dot_general | solution.py:44
  90.9 11.1 %fusion.55 = f32[12,512]{1,0:T(8,128)S(1)} fusion(f32[12,512,512]{1,2,0:T(8,128)} %fusion.32), kind=kOutput, calls=%fused_computation.61 | output fusion | flops 12583423 | bytes 12607488 | tf_op jit(solution)/shard_map/while/body/eval_jaxpr/sub | solution.py:48
  102.1 0.0 all-to-all-done
  102.1 1.3 reshape.104
  103.4 12.5 %fusion.35 = bf16[12,64,512]{2,1,0:T(8,128)(2,1)S(1)} fusion(f32[12,512]{1,0:T(8,128)S(1)} %fusion.55, bf16[512,12,64]{2,1,0:T(8,128)(2,1)S(1)} %reshape.104, f32[12,512,512]{1,2,0:T(8,128)} %fusion.32), kind=kOutput, calls=%fused_computation.43 | convolution fusion | flops 418781696 | bytes 14180352 | tf_op jit(solution)/shard_map/while/body/eval_jaxpr/hqk,khd->qhd/dot_general | solution.py:50
  115.8 1.8 copy.40
  117.7 0.5 broadcast.73
  118.2 0.0 copy-start.1
  118.2 5.5 %reduce = bf16[512,768]{1,0:T(8,128)(2,1)S(1)} reduce(bf16[512,1,1,768]{3,2,1,0:T(2,128)(2,1)S(1)} %bitcast.68, bf16[]{:T(256)} %broadcast.73), dimensions={1,2}, to_apply=%bitcast.56.reduce_sub_computation | reduce | bytes 1572866
  123.7 0.2 reshape.114
  123.9 29.7 %all_to_all.18 = bf16[16,2,12288]{2,1,0:T(2,128)(2,1)S(1)} all-to-all(bf16[16,2,12288]{2,1,0:T(2,128)(2,1)S(1)} %reshape.114), channel_id=1, replica_groups=mesh['tm'=16,'space'=16] {'space'}, dimensions={0} | all-to-all | bytes 1572864 | tf_op jit(solution)/shard_map/all_to_all | solution.py:79
  153.5 0.7 reshape.115
  154.3 0.1 copy.46
  154.4 0.0 copy-done.1
  154.4 2.2 fusion.26
  156.6 0.0 copy-start.2
  156.6 0.2 fusion.27
  156.8 0.7 copy-done.2
  157.5 4.0 %convert_bitcast_fusion = bf16[3,512,768]{2,1,0:T(8,128)(2,1)S(1)} fusion(bf16[512,768,1]{1,0,2:T(8,128)(2,1)S(1)} %bitcast.75, bf16[4,768,768]{2,1,0:T(8,128)(2,1)} %param.5), kind=kOutput, calls=%fused_computation.29 | convolution fusion | flops 1813118976 | bytes 6684672 | tf_op jit(solution)/shard_map/rd,jde->jre/dot_general | solution.py:20
  161.5 1.4 fusion.53
  162.9 0.0 all-gather.5.cloned.1.call-update
  162.9 0.0 all-gather.3.cloned.1.call-start
  162.9 0.7 all-gather.3.cloned.1.call-update
  163.7 0.1 iota_compare_fusion
  163.7 1.5 reshape_reshape_squeeze.15
  165.2 89.3 %all-gather.5.cloned.1.call-done = bf16[256,32,768]{2,1,0:T(8,128)(2,1)} async-done(((bf16[16,32,768]{2,1,0:T(8,128)(2,1)}), bf16[256,32,768]{2,1,0:T(8,128)(2,1)}) %all-gather.5.cloned.1.call-update) | async-done | bytes 12582928 | tf_op jit(solution)/shard_map/all_gather | solution.py:89
  254.5 16.7 %copy.42 = bf16[256,32,768]{0,2,1:T(8,128)(2,1)} copy(bf16[256,32,768]{2,1,0:T(8,128)(2,1)} %all-gather.5.cloned.1.call-done) | data formatting | bytes 25165824 | tf_op jit(solution)/shard_map/all_gather | solution.py:89
  271.1 6.0 %fusion.6 = (f32[16,32,12]{0,2,1:T(8,128)S(1)}, f32[32,12,256,16]{2,3,1,0:T(8,128)S(1)}) fusion(pred[16,256]{1,0:T(8,128)(4,1)S(1)} %iota_compare_fusion, bf16[256,32,12,64]{0,3,2,1:T(8,128)(2,1)} %bitcast.66, bf16[16,32,12,64]{3,2,1,0:T(8,128)(2,1)S(1)} %reshape_reshape_squeeze.15), kind=kOutput, calls=%fused_computation.9 | convolution fusion | flops 206039040 | bytes 19689472 | tf_op jit(solution)/shard_map/fphd,gphd->fphg/dot_general | solution.py:94
  277.2 0.0 copy-start
  277.2 2.7 copy-done
  279.9 2.1 fusion.7
  282.0 69.5 %all-gather.3.cloned.1.call-done = bf16[256,32,768]{2,1,0:T(8,128)(2,1)} async-done(((bf16[16,32,768]{2,1,0:T(8,128)(2,1)}), bf16[256,32,768]{2,1,0:T(8,128)(2,1)}) %all-gather.3.cloned.1.call-update) | async-done | bytes 12582928 | tf_op jit(solution)/shard_map/all_gather | solution.py:90
  351.5 16.7 %copy.41 = bf16[256,32,768]{0,2,1:T(8,128)(2,1)} copy(bf16[256,32,768]{2,1,0:T(8,128)(2,1)} %all-gather.3.cloned.1.call-done) | data formatting | bytes 25165824 | tf_op jit(solution)/shard_map/all_gather | solution.py:90
  368.3 8.3 %fusion.13 = bf16[16,32,12,64]{3,0,2,1:T(8,128)(2,1)S(1)} fusion(f32[16,32,12]{0,2,1:T(8,128)S(1)} %fusion.7, bf16[256,32,12,64]{0,3,2,1:T(8,128)(2,1)} %bitcast.67, f32[32,12,256,16]{2,3,1,0:T(8,128)} %copy-done, f32[16,32,12]{0,2,1:T(8,128)S(1)} %broadcast_maximum_fusion, pred[16,256]{1,0:T(8,128)(4,1)S(1)} %iota_compare_fusion), kind=kOutput, calls=%fused_computation.17 | convolution fusion | flops 208404480 | bytes 19714048 | tf_op jit(solution)/shard_map/fphg,gphd->fphd/dot_general | solution.py:103
  376.6 0.0 copy-start.3
  376.6 0.5 copy.44
  377.1 2.0 convert_element_type.65
  379.2 0.0 copy-done.3
  379.2 3.2 fusion.28
  (4 shorter events, 0.0 us)
Async XLA Ops:
  72.7 29.4 %all-to-all-start = ((bf16[16,1,32,768]{3,2,1,0:T(8,128)(2,1)}), bf16[16,1,32,768]{3,2,1,0:T(8,128)(2,1)S(1)}, u32[]{:S(2)}, u32[]{:S(2)}) async-start(bf16[16,1,32,768]{3,2,1,0:T(8,128)(2,1)} %bitcast.4), calls=%async_computation | async-start | bytes 1572864 | tf_op jit(solution)/shard_map/all_to_all | solution.py:74
  76.2 178.3 %all-gather.5.cloned.1.call-start = ((), (), s32[]{:S(2)}) async-start(), calls=%async_computation.5 | async-start | bytes 13369344 | tf_op jit(solution)/shard_map/all_gather | solution.py:89
  118.2 36.2 %copy-start.1 = (bf16[16,32,768]{2,1,0:T(8,128)(2,1)S(1)}, bf16[16,32,768]{2,1,0:T(8,128)(2,1)}, u32[]{:S(2)}) copy-start(bf16[16,32,768]{2,1,0:T(8,128)(2,1)} %param.3) | copy-start | bytes 2359300
  156.6 0.9 copy-start.2
  162.9 188.6 %all-gather.3.cloned.1.call-start = ((), (), s32[]{:S(2)}) async-start(), calls=%async_computation.4 | async-start | bytes 13369344 | tf_op jit(solution)/shard_map/all_gather | solution.py:90
  277.2 2.7 copy-start
  376.6 2.6 copy-start.3
Sparse Core Ops, SparseCore 0:
  163.0 91.4 all-gather.4
  256.9 94.5 all-gather.2
where the time goes:
time: 391 us; the launch traced here: 389 us
  waiting for transfers between devices  159 us (41%)
  blocking collectives  88 us (23%)
  local copies, waits for them, and re-layouts  54.3 us (14%)
  matrix products  48.2 us (12%)
  other arithmetic  21.7 us (6%)
  between operations  13.6 us (3%)
    all_gather x1, waiting for transfers between devices, on_device(): key_piece = lax.all_gather(tk, 'tm', axis=0, tiled=True)  89.3 us
    all_gather x1, waiting for transfers between devices, on_device(): value_piece = lax.all_gather(tv, 'tm', axis=0, tiled=True)  69.5 us
    all_to_all x1, blocking collectives, on_device(): lax.all_to_all(sq.reshape(frame_shape), 'space', split_axis=0, concat_axi...  32.7 us
    all_to_all x1, blocking collectives, on_device(): lax.all_to_all(smix, 'space', split_axis=2, concat_axis=0, tiled=True)  29.7 us
    all_to_all x1, blocking collectives, on_device(): lax.all_to_all(sk.reshape(frame_shape), 'space', split_axis=0, concat_axi...  25.7 us
    all_gather x1, local copies, waits for them, and re-layouts, on_device(): value_piece = lax.all_gather(tv, 'tm', axis=0, tiled=True)  16.7 us
    all_gather x1, local copies, waits for them, and re-layouts, on_device(): key_piece = lax.all_gather(tk, 'tm', axis=0, tiled=True)  16.7 us
    dot_general x1, matrix products, attend_frame(): jnp.einsum('hqk,khd->qhd', weights, vh, preferred_element_type=jnp.float32)  12.5 us
  transfers between devices with their start and end apart: 3, of which 2 were waited for; matrix products, arithmetic and copies ran while one was open for 13% of the time, Pallas kernels for 0%

commit v1 on v0

--- a/solution.py
+++ b/solution.py
@@ -1,3 +1,4 @@
+import functools
 import math
 import jax
 import jax.numpy as jnp
@@ -5,6 +6,22 @@
 from jax.sharding import PartitionSpec as P
 
 HEAD = 64
+
+
+def handle_joints(array_in, dim_no):
+    w1 = jnp.concatenate(
+        jax.lax.all_to_all(
+            jnp.stack([array_in for _ in range(jax.lax.axis_size("tm"))]),
+            split_axis=0,
+            axis_name="tm",
+            concat_axis=0,
+        ),
+        axis=dim_no,
+    )
+    return w1
+
+
+shape_positions_up = functools.partial(handle_joints, dim_no=0)
 
 
 def rms_norm(values):
@@ -87,7 +104,7 @@
     query_pos = first_frame + jnp.arange(frames, dtype=jnp.int32)
     running = jnp.full((frames, toks, heads), -1e30, jnp.float32)
     key_piece = lax.all_gather(tk, "tm", axis=0, tiled=True)
-    value_piece = lax.all_gather(tv, "tm", axis=0, tiled=True)
+    value_piece = shape_positions_up(tv)
     count = key_piece.shape[0]
     kh = key_piece.reshape(count, toks, heads, HEAD)
     vh = value_piece.reshape(count, toks, heads, HEAD)

time: 391 us -> 510 us (1.30); the launches traced: 389 us -> 501 us
  waiting for transfers between devices: 159 us -> 229 us
  local copies, waits for them, and re-layouts: 54.3 us -> 81.5 us
  matrix products: 48.2 us -> 56.4 us
  starting transfers between devices: 3.78 us -> 10.5 us
    all_to_all x0 -> x1, waiting for transfers between devices: none -> 229 us  [handle_joints(): jax.lax.all_to_all(jnp.stack([array_in for _ in range(jax.lax.axis_size('...]
    all_gather x1, waiting for transfers between devices: 89.3 us -> 0.01 us  [on_device(): key_piece = lax.all_gather(tk, 'tm', axis=0, tiled=True)]
    all_gather x1 -> x0, waiting for transfers between devices: 69.5 us -> none  [on_device(): value_piece = lax.all_gather(tv, 'tm', axis=0, tiled=True)]
    another operation x0 -> x2, local copies, waits for them, and re-layouts: none -> 44.4 us  [the longest x1 38.3 us: on_device(): vh = value_piece.reshape(count, toks, heads, HEAD)]
    all_gather x1 -> x0, local copies, waits for them, and re-layouts: 16.7 us -> none  [on_device(): value_piece = lax.all_gather(tv, 'tm', axis=0, tiled=True)]
    dot_general x1, matrix products: 8.34 us -> 16.6 us  [on_device(): acc = jnp.einsum('fphg,gphd->fphd', expo, vh.astype(jnp.float32))]
    all_to_all x1, blocking collectives: 25.7 us -> 32.7 us  [on_device(): lax.all_to_all(sk.reshape(frame_shape), 'space', split_axis=0, concat_axi...]
    all_to_all x1, blocking collectives: 32.7 us -> 25.7 us  [on_device(): lax.all_to_all(sq.reshape(frame_shape), 'space', split_axis=0, concat_axi...]
  transfers between devices with their start and end apart: 3 -> 3, of which waited for: 2 -> 1; matrix products, arithmetic and copies ran while one was open for 13% -> 14% of each run, Pallas kernels for 0% -> 0%
where the time goes in v1:
time: 510 us; the launch traced here: 501 us
  waiting for transfers between devices  229 us (45%)
  blocking collectives  88 us (17%)
  local copies, waits for them, and re-layouts  81.5 us (16%)
  matrix products  56.4 us (11%)
  other arithmetic  21.8 us (4%)
  between operations  13.6 us (3%)
  starting transfers between devices  10.5 us (2%)
    all_to_all x1, waiting for transfers between devices, handle_joints(): jax.lax.all_to_all(jnp.stack([array_in for _ in range(jax.lax.axis_size('...  229 us
    another operation x1, local copies, waits for them, and re-layouts, on_device(): vh = value_piece.reshape(count, toks, heads, HEAD)  38.3 us
    all_to_all x1, blocking collectives, on_device(): lax.all_to_all(sk.reshape(frame_shape), 'space', split_axis=0, concat_axi...  32.7 us
    all_to_all x1, blocking collectives, on_device(): lax.all_to_all(smix, 'space', split_axis=2, concat_axis=0, tiled=True)  29.7 us
    all_to_all x1, blocking collectives, on_device(): lax.all_to_all(sq.reshape(frame_shape), 'space', split_axis=0, concat_axi...  25.7 us
    all_gather x1, local copies, waits for them, and re-layouts, on_device(): key_piece = lax.all_gather(tk, 'tm', axis=0, tiled=True)  16.8 us
    dot_general x1, matrix products, on_device(): acc = jnp.einsum('fphg,gphd->fphd', expo, vh.astype(jnp.float32))  16.6 us
    dot_general x1, matrix products, attend_frame(): jnp.einsum('hqk,khd->qhd', weights, vh, preferred_element_type=jnp.float32)  12.5 us
  transfers between devices with their start and end apart: 3, of which 1 were waited for; matrix products, arithmetic and copies ran while one was open for 14% of the time, Pallas kernels for 0%

profile of v1, /device:TPU:1, one launch (start us, length us, event | category | flops | bytes accessed | tf_op | source)
XLA Modules:
  0.0 500.8 jit_solution(13046796380715723492)
XLA Ops:
  6.5 1.4 fusion.24
  7.9 1.3 fusion.25
  9.2 4.0 convert_bitcast_fusion.1
  13.3 1.0 fusion.57
  14.3 32.7 %all_to_all.20 = bf16[16,1,32,768]{3,2,1,0:T(8,128)(2,1)} all-to-all(bf16[16,1,32,768]{3,2,1,0:T(8,128)(2,1)S(1)} %bitcast.72), channel_id=1, replica_groups=mesh['tm'=16,'space'=16] {'space'}, dimensions={0} | all-to-all | bytes 1572864 | tf_op jit(solution)/shard_map/all_to_all | solution.py:88
  47.0 25.7 %all_to_all.42 = bf16[16,1,32,768]{3,2,1,0:T(8,128)(2,1)} all-to-all(bf16[16,1,32,768]{3,2,1,0:T(8,128)(2,1)S(1)} %bitcast.71), channel_id=1, replica_groups=mesh['tm'=16,'space'=16] {'space'}, dimensions={0} | all-to-all | bytes 1572864 | tf_op jit(solution)/shard_map/all_to_all | solution.py:85
  72.7 3.5 all-to-all-start
  76.2 0.2 all-gather.2.cloned.1.call-start
  76.4 2.7 reshape.104
  79.1 3.8 reshape.105
  82.9 8.0 %fusion.33 = f32[12,512,512]{1,2,0:T(8,128)} fusion(bf16[512,12,64]{2,1,0:T(8,128)(2,1)} %reshape.105, bf16[512,12,64]{2,1,0:T(8,128)(2,1)S(1)} %reshape.104), kind=kOutput, calls=%fused_computation.41 | convolution fusion | flops 402653184 | bytes 14155776 | tf_op jit(solution)/shard_map/while/body/eval_jaxpr/qhd,khd->hqk/dot_general | solution.py:61
  90.9 11.1 %fusion.58 = f32[12,512]{1,0:T(8,128)S(1)} fusion(f32[12,512,512]{1,2,0:T(8,128)} %fusion.33), kind=kOutput, calls=%fused_computation.62 | output fusion | flops 12583423 | bytes 12607488 | tf_op jit(solution)/shard_map/while/body/eval_jaxpr/sub | solution.py:65
  102.1 0.0 all-to-all-done
  102.1 1.3 reshape.103
  103.4 12.5 %fusion.36 = bf16[12,64,512]{2,1,0:T(8,128)(2,1)S(1)} fusion(f32[12,512]{1,0:T(8,128)S(1)} %fusion.58, bf16[512,12,64]{2,1,0:T(8,128)(2,1)S(1)} %reshape.103, f32[12,512,512]{1,2,0:T(8,128)} %fusion.33), kind=kOutput, calls=%fused_computation.44 | convolution fusion | flops 418781696 | bytes 14180352 | tf_op jit(solution)/shard_map/while/body/eval_jaxpr/hqk,khd->qhd/dot_general | solution.py:67
  115.8 1.8 copy.40
  117.7 0.5 broadcast.74
  118.2 0.0 copy-start.1
  118.2 5.5 %reduce = bf16[512,768]{1,0:T(8,128)(2,1)S(1)} reduce(bf16[512,1,1,768]{3,2,1,0:T(2,128)(2,1)S(1)} %bitcast.67, bf16[]{:T(256)} %broadcast.74), dimensions={1,2}, to_apply=%bitcast.57.reduce_sub_computation | reduce | bytes 1572866
  123.7 0.2 reshape.112
  123.9 29.7 %all_to_all.43 = bf16[16,2,12288]{2,1,0:T(2,128)(2,1)S(1)} all-to-all(bf16[16,2,12288]{2,1,0:T(2,128)(2,1)S(1)} %reshape.112), channel_id=1, replica_groups=mesh['tm'=16,'space'=16] {'space'}, dimensions={0} | all-to-all | bytes 1572864 | tf_op jit(solution)/shard_map/all_to_all | solution.py:96
  153.5 0.7 reshape.113
  154.3 0.1 copy.46
  154.4 0.0 copy-done.1
  154.4 2.2 fusion.27
  156.6 0.0 copy-start.2
  156.6 0.2 fusion.28
  156.8 0.7 copy-done.2
  157.5 4.0 convert_bitcast_fusion
  161.5 1.1 fusion.56
  162.5 0.0 all-gather.2.cloned.1.call-update
  162.6 6.2 %stack.3 = bf16[16,16,32,768]{3,2,1,0:T(8,128)(2,1)} broadcast(bf16[16,32,768]{2,1,0:T(8,128)(2,1)S(1)} %bitcast.69), dimensions={1,2,3} | broadcast | bytes 13369344 | tf_op jit(solution)/shard_map/stack | solution.py:14
  168.7 6.8 %all-to-all-start.4 = ((bf16[16,16,32,768]{3,2,1,0:T(8,128)(2,1)}), bf16[16,16,32,768]{3,2,1,0:T(8,128)(2,1)}, u32[]{:S(2)}, u32[]{:S(2)}) async-start(bf16[16,16,32,768]{3,2,1,0:T(8,128)(2,1)} %stack.3), calls=%async_computation.4 | async-start | bytes 25165824 | tf_op jit(solution)/shard_map/all_to_all | solution.py:13
  175.6 0.1 iota_compare_fusion
  175.6 1.3 reshape_reshape_squeeze.15
  176.9 228.8 %all-to-all-done.4 = bf16[16,16,32,768]{3,2,1,0:T(8,128)(2,1)} async-done(((bf16[16,16,32,768]{3,2,1,0:T(8,128)(2,1)}), bf16[16,16,32,768]{3,2,1,0:T(8,128)(2,1)}, u32[]{:S(2)}, u32[]{:S(2)}) %all-to-all-start.4) | async-done | bytes 12582944 | tf_op jit(solution)/shard_map/all_to_all | solution.py:13
  405.7 38.3 %reshape_reshape.4 = bf16[256,32,12,64]{3,2,1,0:T(8,128)(2,1)} reshape(bf16[16,16,32,768]{3,2,1,0:T(8,128)(2,1)} %all-to-all-done.4) | data formatting | bytes 25165824 | tf_op jit(solution)/shard_map/reshape;reshape | solution.py:110
  444.0 0.0 all-gather.2.cloned.1.call-done
  444.0 16.8 %copy.41 = bf16[256,32,768]{0,2,1:T(8,128)(2,1)} copy(bf16[256,32,768]{2,1,0:T(8,128)(2,1)} %all-gather.2.cloned.1.call-done) | data formatting | bytes 25165824 | tf_op jit(solution)/shard_map/all_gather | solution.py:106
  460.8 6.0 %fusion.8 = (f32[16,32,12]{0,2,1:T(8,128)S(1)}, f32[32,12,256,16]{2,3,1,0:T(8,128)S(1)}) fusion(pred[16,256]{1,0:T(8,128)(4,1)S(1)} %iota_compare_fusion, bf16[256,32,12,64]{0,3,2,1:T(8,128)(2,1)} %bitcast.66, bf16[16,32,12,64]{3,2,1,0:T(8,128)(2,1)S(1)} %reshape_reshape_squeeze.15), kind=kOutput, calls=%fused_computation.11 | convolution fusion | flops 206039040 | bytes 19689472 | tf_op jit(solution)/shard_map/fphd,gphd->fphg/dot_general | solution.py:111
  466.9 0.0 copy-start
  466.9 2.5 copy-done
  469.5 2.1 fusion.9
  471.6 16.6 %fusion.14 = bf16[16,32,12,64]{3,0,2,1:T(8,128)(2,1)S(1)} fusion(f32[16,32,12]{0,2,1:T(8,128)S(1)} %fusion.9, f32[32,12,256,16]{2,3,1,0:T(8,128)} %copy-done, f32[16,32,12]{0,2,1:T(8,128)S(1)} %broadcast_maximum_fusion, pred[16,256]{1,0:T(8,128)(4,1)S(1)} %iota_compare_fusion, bf16[256,32,12,64]{3,2,1,0:T(8,128)(2,1)} %reshape_reshape.4), kind=kOutput, calls=%fused_computation.18 | convolution fusion | flops 208404480 | bytes 19714048 | tf_op jit(solution)/shard_map/fphg,gphd->fphd/dot_general | solution.py:120
  488.2 0.0 copy-start.3
  488.2 0.5 copy.44
  488.7 2.0 convert_element_type.65
  490.8 0.0 copy-done.3
  490.8 3.2 fusion.29
  (4 shorter events, 0.0 us)
Async XLA Ops:
  72.7 29.4 %all-to-all-start = ((bf16[16,1,32,768]{3,2,1,0:T(8,128)(2,1)}), bf16[16,1,32,768]{3,2,1,0:T(8,128)(2,1)S(1)}, u32[]{:S(2)}, u32[]{:S(2)}) async-start(bf16[16,1,32,768]{3,2,1,0:T(8,128)(2,1)} %bitcast.4), calls=%async_computation | async-start | bytes 1572864 | tf_op jit(solution)/shard_map/all_to_all | solution.py:91
  76.2 367.8 %all-gather.2.cloned.1.call-start = ((), (), s32[]{:S(2)}) async-start(), calls=%async_computation.5 | async-start | bytes 13369344 | tf_op jit(solution)/shard_map/all_gather | solution.py:106
  118.2 36.2 %copy-start.1 = (bf16[16,32,768]{2,1,0:T(8,128)(2,1)S(1)}, bf16[16,32,768]{2,1,0:T(8,128)(2,1)}, u32[]{:S(2)}) copy-start(bf16[16,32,768]{2,1,0:T(8,128)(2,1)} %param.3) | copy-start | bytes 2359300
  156.6 0.9 copy-start.2
  168.7 237.0 %all-to-all-start.4 = ((bf16[16,16,32,768]{3,2,1,0:T(8,128)(2,1)}), bf16[16,16,32,768]{3,2,1,0:T(8,128)(2,1)}, u32[]{:S(2)}, u32[]{:S(2)}) async-start(bf16[16,16,32,768]{3,2,1,0:T(8,128)(2,1)} %stack.3), calls=%async_computation.4 | async-start | bytes 25165824 | tf_op jit(solution)/shard_map/all_to_all | solution.py:13
  466.9 2.6 copy-start
  488.2 2.6 copy-start.3
Sparse Core Ops, SparseCore 0:
  162.7 273.7 all-gather.1
